TPU v7x, 32 devices: a whole 2x2x4 slice. The times are simulated.
32 devices in a mesh: space: 4 (over y, x), vel: 8 (over z, core).
Axes of the slice: x: 2, y: 2, z: 4, core: 2. Of those that a mesh axis runs over, the one named last changes fastest.
Arguments:
- cotangent: float32 [8192, 128, 128], P('vel', 'space'), may hold values from -6 to 6
- speed: float32 [3, 8192], P(None, 'vel'), may hold values from 0.1 to 3
- direction: int32 [3, 8192], P(None, 'vel'), may hold values from 0 to 1
- macroscopic_record: float32 [3, 5, 128, 128], P(None, None, 'space'), may hold values from -1 to 2, as said below
Outputs:
- gradient: float32 [8192, 128, 128], P('vel', 'space')
Inputs may be any that keep to these rules, and one draw needn't show every extreme that they name: `direction`: 1 marks a positive velocity component, 0 a negative one. `macroscopic_record`: density and temperature lie between 0.5 and 2, flow velocity components between -1 and 1.
All inputs are finite; a program needn't handle non-finite values.
Results may differ from a plain program's by a relative error of at most 0.00013.
Values sent between devices are 32-bit elements; how exact they have to be, the bound alone decides.
No kernel may reach another device: no remote copies, remote signals or barrier semaphores. Data moves between devices by JAX's collectives and lax.ppermute only.
A program may use at most 128 MiB of HBM per device.

v0:
```python
import math
import jax
import jax.numpy as jnp
from jax import lax
from jax.sharding import PartitionSpec as P

SPEED_POINTS = 8192
STEPS = 3
courant_number = 0.1
region_capacity = 216.0
mode_gains = (
    1.0,
    1.0,
    1.0,
    1.0,
    1.0,
    -0.5,
    -0.5,
    -0.5,
    -0.5,
    -0.5,
    1.0 / 3.0,
    1.0 / 3.0,
    1.0 / 3.0,
)
monomials = [
    (first, second, degree - first - second)
    for degree in range(4)
    for first in range(degree, -1, -1)
    for second in range(degree - first, -1, -1)
]
monomial_place = {exponents: place for place, exponents in enumerate(monomials)}


def with_halo(x, sides, width):
    for axis, dim in sides:
        peers, length = (lax.axis_size(axis), x.shape[dim])
        up = [(i, (i + 1) % peers) for i in range(peers)]
        down = [(j, i) for i, j in up]
        last = lax.slice_in_dim(x, length - width, length, axis=dim)
        first = lax.slice_in_dim(x, 0, width, axis=dim)
        before = lax.ppermute(last, axis, up)
        after = lax.ppermute(first, axis, down)
        x = jnp.concatenate([before, x, after], axis=dim)
    return x


def raise_to(values, exponent):
    result = jnp.ones_like(values)
    for repeat in range(exponent):
        result = result * values
    return result


def poly_mul(left, right):
    result = {}
    for left_key, left_coef in left.items():
        for right_key, right_coef in right.items():
            joined = (
                left_key[0] + right_key[0],
                left_key[1] + right_key[1],
                left_key[2] + right_key[2],
            )
            product = left_coef * right_coef
            result[joined] = result[joined] + product if joined in result else product
    return result


def poly_comb(terms):
    result = {}
    for weight, poly in terms:
        for poly_key, poly_coef in poly.items():
            scaled = weight * poly_coef
            result[poly_key] = result[poly_key] + scaled if poly_key in result else scaled
    return result


def hermite_polys(flow_rows, reciprocal_factor):
    linear = []
    for component in range(3):
        unit_key = tuple((1 if other == component else 0 for other in range(3)))
        linear.append(
            {unit_key: reciprocal_factor, (0, 0, 0): -flow_rows[component] * reciprocal_factor}
        )
    comp_x, comp_y, comp_z = linear
    unit_poly = {(0, 0, 0): 1.0}
    square_x = poly_mul(comp_x, comp_x)
    square_y = poly_mul(comp_y, comp_y)
    square_z = poly_mul(comp_z, comp_z)
    square = poly_comb([(1.0, square_x), (1.0, square_y), (1.0, square_z)])
    shifted = poly_comb([(1.0, square), (-5.0, unit_poly)])
    heat_scale = 1.0 / math.sqrt(10.0)
    return [
        unit_poly,
        comp_x,
        comp_y,
        comp_z,
        poly_comb([(1.0 / math.sqrt(6.0), square), (-3.0 / math.sqrt(6.0), unit_poly)]),
        poly_mul(comp_x, comp_y),
        poly_mul(comp_x, comp_z),
        poly_mul(comp_y, comp_z),
        poly_comb([(0.5, square_x), (-0.5, square_y)]),
        poly_comb(
            [
                (1.0 / math.sqrt(12.0), square_x),
                (1.0 / math.sqrt(12.0), square_y),
                (-2.0 / math.sqrt(12.0), square_z),
            ]
        ),
        poly_comb([(heat_scale, poly_mul(comp_x, shifted))]),
        poly_comb([(heat_scale, poly_mul(comp_y, shifted))]),
        poly_comb([(heat_scale, poly_mul(comp_z, shifted))]),
    ]


def to_modes(raw_rows, polys, zeros_like):
    mode_rows = []
    for poly in polys:
        running = zeros_like
        for poly_key, poly_coef in poly.items():
            running = running + poly_coef * raw_rows[monomial_place[poly_key]]
        mode_rows.append(running)
    return mode_rows


def to_coeffs(mode_rows, polys, zeros_like):
    coeff_rows = [zeros_like for exponents in monomials]
    for mode_index, poly in enumerate(polys):
        scaled_mode = mode_gains[mode_index] * mode_rows[mode_index]
        for poly_key, poly_coef in poly.items():
            place = monomial_place[poly_key]
            coeff_rows[place] = coeff_rows[place] + poly_coef * scaled_mode
    return jnp.stack(coeff_rows)


def pad_both(values, along):
    extent = values.shape[along]
    lower_rim = lax.slice_in_dim(values, extent - 2, extent, axis=along)
    upper_rim = lax.slice_in_dim(values, 0, 2, axis=along)
    return jnp.concatenate([lower_rim, values, upper_rim], axis=along)


def upwind_back(padded, length, along, lam_col, positive):

    def window(start_at):
        return lax.slice_in_dim(padded, start_at, start_at + length, axis=along)

    center = window(2)
    nearer = jnp.where(positive, window(3), window(1))
    farther = jnp.where(positive, window(4), window(0))
    return center - 0.5 * lam_col * (3.0 * center - 4.0 * nearer + farther)


def shards(cotangent, speed, direction, macroscopic_record):
    rows_x = cotangent.shape[1]
    cols_y = cotangent.shape[2]
    velocity = (2 * direction - 1).astype(jnp.float32) * speed
    factors = courant_number * speed
    positive = direction > 0
    lam_x = factors[0][:, None, None]
    lam_y = factors[1][:, None, None]
    pos_x = positive[0][:, None, None]
    pos_y = positive[1][:, None, None]
    table = jnp.stack(
        [
            raise_to(velocity[0], exponents[0])
            * raise_to(velocity[1], exponents[1])
            * raise_to(velocity[2], exponents[2])
            for exponents in monomials
        ]
    )
    adjoint = cotangent
    for iteration_counter in range(STEPS - 1, -1, -1):
        moved_y = upwind_back(pad_both(adjoint, 2), cols_y, 2, lam_y, pos_y)
        padded_x = with_halo(moved_y, (("space", 1),), 2)
        advected = upwind_back(padded_x, rows_x, 1, lam_x, pos_x)
        particle_concentration = macroscopic_record[iteration_counter, 0]
        flow_rows = [macroscopic_record[iteration_counter, 1 + component] for component in range(3)]
        thermal_energy_level = macroscopic_record[iteration_counter, 4]
        reciprocal_factor = 1.0 / jnp.sqrt(thermal_energy_level)
        normalising_coefficient = (
            particle_concentration
            * (2.0 * math.pi * thermal_energy_level) ** (-1.5)
            * region_capacity
            / SPEED_POINTS
        )
        relaxation_rate = 0.3 * particle_concentration * jnp.sqrt(thermal_energy_level)
        peculiar = [
            (velocity[component][:, None, None] - flow_rows[component]) * reciprocal_factor
            for component in range(3)
        ]
        weight = normalising_coefficient * jnp.exp(
            -0.5 * (peculiar[0] ** 2 + peculiar[1] ** 2 + peculiar[2] ** 2)
        )
        raw_moments = jnp.einsum(
            "av,vxy->axy", table, weight * advected, precision=lax.Precision.HIGHEST
        )
        zero_cells = jnp.zeros_like(particle_concentration)
        summed = lax.psum(raw_moments, "vel")
        polys = hermite_polys(flow_rows, reciprocal_factor)
        coeffs = to_coeffs(to_modes(summed, polys, zero_cells), polys, zero_cells)
        returned = jnp.einsum("av,axy->vxy", table, coeffs, precision=lax.Precision.HIGHEST)
        adjoint = (1.0 - relaxation_rate) * advected + relaxation_rate * returned
    return adjoint


def solution(mesh):
    in_specs = (
        P("vel", "space", None),
        P(None, "vel"),
        P(None, "vel"),
        P(None, None, "space", None),
    )
    out_specs = P("vel", "space", None)
    return jax.shard_map(shards, mesh=mesh, in_specs=in_specs, out_specs=out_specs, check_vma=False)
```

profile of v0, /device:TPU:0, one launch (start us, length us, event | category | flops | bytes accessed | tf_op | source)
XLA Modules:
  0.0 712.7 jit_solution(4509849928719995497)
XLA Ops:
  8.0 16.5 %copy.21 = f32[1024,32,128]{0,2,1:T(8,128)} copy(f32[1024,32,128]{2,1,0:T(8,128)} %param.4) | data formatting | bytes 33554432 | tf_op args[0]
  26.9 34.9 %fusion.46 = f32[1024,32,128]{0,2,1:T(8,128)} fusion(f32[1024,32,128]{0,2,1:T(8,128)} %copy.21, f32[1024,32,2]{0,2,1:T(2,128)S(1)} %get-tuple-element.47, f32[1024,32,2]{0,2,1:T(2,128)S(1)} %get-tuple-element.46, f32[1024]{0:T(1024)S(1)} %bitcast.1794, pred[1024]{0:T(1024)(128)(4,1)S(1)} %get-tuple-element.6), kind=kLoop, calls=%fused_computation.70 | loop fusion | flops 50331648 | bytes 34083840 | tf_op jit(solution)/shard_map/sub | solution.py:151
  71.3 21.0 %collective-permute-done = f32[1024,2,128]{0,2,1:T(8,128)S(1)} collective-permute-done((f32[1024,2,128]{0,2,1:T(8,128)}, f32[1024,2,128]{0,2,1:T(8,128)S(1)}, u32[]{:S(2)}, u32[]{:S(2)}) %collective-permute-start) | collective-permute-done | bytes 1048608 | tf_op jit(solution)/shard_map/ppermute | solution.py:43
  92.3 22.2 %collective-permute-done.1 = f32[1024,2,128]{0,2,1:T(8,128)S(1)} collective-permute-done((f32[1024,2,128]{0,2,1:T(8,128)S(1)}, f32[1024,2,128]{0,2,1:T(8,128)S(1)}, u32[]{:S(2)}, u32[]{:S(2)}) %collective-permute-start.1) | collective-permute-done | bytes 1048608 | tf_op jit(solution)/shard_map/ppermute | solution.py:42
  114.6 27.7 %fusion.38 = f32[1024,32,128]{0,2,1:T(8,128)S(1)} fusion(f32[1024,32,128]{0,2,1:T(8,128)} %fusion.46, f32[1024,2,128]{0,2,1:T(8,128)S(1)} %collective-permute-done.1, f32[1024,2,128]{0,2,1:T(8,128)S(1)} %collective-permute-done, f32[1024]{0:T(1024)S(1)} %bitcast.1791, pred[1024]{0:T(1024)(128)(4,1)S(1)} %get-tuple-element.5), kind=kLoop, calls=%fused_computation.62 | loop fusion | flops 50331648 | bytes 35656704 | tf_op jit(solution)/shard_map/sub | solution.py:151
  142.3 23.4 %fusion.86 = f32[20,32,128]{2,0,1:T(8,128)S(1)} fusion(f32[1024,32,128]{0,2,1:T(8,128)S(1)} %fusion.38, f32[32,128]{1,0:T(8,128)S(1)} %get-tuple-element.55, f32[1024]{0:T(1024)S(1)} %bitcast.1803, f32[32,128]{1,0:T(8,128)S(1)} %get-tuple-element.56, f32[1024]{0:T(1024)S(1)} %bitcast.1800, f32[32,128]{1,0:T(8,128)S(1)} %get-tuple-element.58, ...), kind=kOutput, calls=%fused_computation.125 | convolution fusion | flops 1065353216 | bytes 17281024 | tf_op jit(solution)/shard_map/av,vxy->axy/dot_general | solution.py:195
  167.0 55.6 %all-reduce.4.cloned.1.call-done = f32[20,32,128]{2,1,0:T(8,128)} async-done(((f32[20,32,128]{2,1,0:T(8,128)}), f32[20,32,128]{2,1,0:T(8,128)}) %all-reduce.4.cloned.1.call-update) | async-done | bytes 327696 | tf_op jit(solution)/shard_map/psum | solution.py:199
  229.0 17.5 %multiply_add_fusion.2 = f32[1024,32,128]{0,2,1:T(8,128)S(1)} fusion(f32[1024,32,128]{0,2,1:T(8,128)} %copy-done.2, f32[32,128]{1,0:T(8,128)S(1)} %get-tuple-element.64, f32[32,128]{1,0:T(8,128)S(1)} %get-tuple-element.63, f32[20,32,128]{2,1,0:T(8,128)S(1)} %constant_dynamic-update-slice_fusion, f32[20,1024]{1,0:T(8,128)S(1)} %stack.12), kind=kOutput, calls=%fused_computation.124 | convolution fusion | flops 1019215872 | bytes 33996800 | tf_op jit(solution)/shard_map/av,axy->vxy/dot_general | solution.py:202
  252.9 34.8 %fusion.30 = f32[1024,32,128]{0,2,1:T(8,128)} fusion(f32[1024,32,128]{0,2,1:T(8,128)} %copy-done.1, f32[1024,32,2]{0,2,1:T(2,128)S(1)} %get-tuple-element.43, f32[1024,32,2]{0,2,1:T(2,128)S(1)} %get-tuple-element.42, f32[1024]{0:T(1024)S(1)} %bitcast.1795, pred[1024]{0:T(1024)(128)(4,1)S(1)} %get-tuple-element.6), kind=kLoop, calls=%fused_computation.54 | loop fusion | flops 50331648 | bytes 34083840 | tf_op jit(solution)/shard_map/sub | solution.py:151
  292.0 23.4 %collective-permute-done.2 = f32[1024,2,128]{0,2,1:T(8,128)S(1)} collective-permute-done((f32[1024,2,128]{0,2,1:T(8,128)S(1)}, f32[1024,2,128]{0,2,1:T(8,128)S(1)}, u32[]{:S(2)}, u32[]{:S(2)}) %collective-permute-start.2) | collective-permute-done | bytes 1048608 | tf_op jit(solution)/shard_map/ppermute | solution.py:43
  315.4 20.5 %collective-permute-done.3 = f32[1024,2,128]{0,2,1:T(8,128)S(1)} collective-permute-done((f32[1024,2,128]{0,2,1:T(8,128)S(1)}, f32[1024,2,128]{0,2,1:T(8,128)S(1)}, u32[]{:S(2)}, u32[]{:S(2)}) %collective-permute-start.3) | collective-permute-done | bytes 1048608 | tf_op jit(solution)/shard_map/ppermute | solution.py:42
  335.9 27.7 %fusion.22 = f32[1024,32,128]{0,2,1:T(8,128)S(1)} fusion(f32[1024,32,128]{0,2,1:T(8,128)} %fusion.30, f32[1024,2,128]{0,2,1:T(8,128)S(1)} %collective-permute-done.3, f32[1024,2,128]{0,2,1:T(8,128)S(1)} %collective-permute-done.2, f32[1024]{0:T(1024)S(1)} %bitcast.1792, pred[1024]{0:T(1024)(128)(4,1)S(1)} %get-tuple-element.5), kind=kLoop, calls=%fused_computation.46 | loop fusion | flops 50331648 | bytes 35656704 | tf_op jit(solution)/shard_map/sub | solution.py:151
  363.7 23.4 %fusion.70 = f32[20,32,128]{2,0,1:T(8,128)S(1)} fusion(f32[1024,32,128]{0,2,1:T(8,128)S(1)} %fusion.22, f32[32,128]{1,0:T(8,128)S(1)} %copy-done.9, f32[32,128]{1,0:T(8,128)S(1)} %copy-done.10, f32[32,128]{1,0:T(8,128)S(1)} %copy-done.12, f32[32,128]{1,0:T(8,128)S(1)} %copy-done.11, f32[32,128]{1,0:T(8,128)S(1)} %copy-done.8, f32[1024]{0:T(1024)S(1)} %bitcast.1804, ...), kind=kOutput, calls=%fused_computation.108 | convolution fusion | flops 1065353216 | bytes 17281024 | tf_op jit(solution)/shard_map/av,vxy->axy/dot_general | solution.py:195
  388.1 54.6 %all-reduce.6.cloned.1.call-done = f32[20,32,128]{2,1,0:T(8,128)} async-done(((f32[20,32,128]{2,1,0:T(8,128)}), f32[20,32,128]{2,1,0:T(8,128)}) %all-reduce.6.cloned.1.call-update) | async-done | bytes 327696 | tf_op jit(solution)/shard_map/psum | solution.py:199
  449.1 17.5 %multiply_add_fusion.1 = f32[1024,32,128]{0,2,1:T(8,128)S(1)} fusion(f32[1024,32,128]{0,2,1:T(8,128)} %copy-done.4, f32[32,128]{1,0:T(8,128)S(1)} %get-tuple-element.66, f32[32,128]{1,0:T(8,128)S(1)} %get-tuple-element.65, f32[20,32,128]{2,1,0:T(8,128)S(1)} %constant_dynamic-update-slice_fusion.20, f32[20,1024]{1,0:T(8,128)S(1)} %stack.12), kind=kOutput, calls=%fused_computation.107 | convolution fusion | flops 1019215872 | bytes 33996800 | tf_op jit(solution)/shard_map/av,axy->vxy/dot_general | solution.py:202
  466.6 6.2 copy-done
  473.0 34.8 %fusion.14 = f32[1024,32,128]{0,2,1:T(8,128)} fusion(f32[1024,32,128]{0,2,1:T(8,128)} %copy-done, f32[1024,32,2]{0,2,1:T(2,128)S(1)} %get-tuple-element.39, f32[1024,32,2]{0,2,1:T(2,128)S(1)} %get-tuple-element.38, f32[1024]{0:T(1024)S(1)} %bitcast.1796, pred[1024]{0:T(1024)(128)(4,1)S(1)} %get-tuple-element.6), kind=kLoop, calls=%fused_computation.38 | loop fusion | flops 50331648 | bytes 34083840 | tf_op jit(solution)/shard_map/sub | solution.py:151
  512.2 23.4 %collective-permute-done.4 = f32[1024,2,128]{0,2,1:T(8,128)S(1)} collective-permute-done((f32[1024,2,128]{0,2,1:T(8,128)S(1)}, f32[1024,2,128]{0,2,1:T(8,128)S(1)}, u32[]{:S(2)}, u32[]{:S(2)}) %collective-permute-start.4) | collective-permute-done | bytes 1048608 | tf_op jit(solution)/shard_map/ppermute | solution.py:43
  535.6 20.5 %collective-permute-done.5 = f32[1024,2,128]{0,2,1:T(8,128)S(1)} collective-permute-done((f32[1024,2,128]{0,2,1:T(8,128)S(1)}, f32[1024,2,128]{0,2,1:T(8,128)S(1)}, u32[]{:S(2)}, u32[]{:S(2)}) %collective-permute-start.5) | collective-permute-done | bytes 1048608 | tf_op jit(solution)/shard_map/ppermute | solution.py:42
  556.1 27.7 %fusion.6 = f32[1024,32,128]{0,2,1:T(8,128)S(1)} fusion(f32[1024,32,128]{0,2,1:T(8,128)} %fusion.14, f32[1024,2,128]{0,2,1:T(8,128)S(1)} %collective-permute-done.5, f32[1024,2,128]{0,2,1:T(8,128)S(1)} %collective-permute-done.4, f32[1024]{0:T(1024)S(1)} %bitcast.1793, pred[1024]{0:T(1024)(128)(4,1)S(1)} %get-tuple-element.5), kind=kLoop, calls=%fused_computation.30 | loop fusion | flops 50331648 | bytes 35656704 | tf_op jit(solution)/shard_map/sub | solution.py:151
  583.8 23.4 %fusion.54 = f32[20,32,128]{2,0,1:T(8,128)S(1)} fusion(f32[1024,32,128]{0,2,1:T(8,128)S(1)} %fusion.6, f32[32,128]{1,0:T(8,128)S(1)} %copy-done.6, f32[32,128]{1,0:T(8,128)S(1)} %copy-done.7, f32[32,128]{1,0:T(8,128)S(1)} %get-tuple-element.60, f32[32,128]{1,0:T(8,128)S(1)} %get-tuple-element.51, f32[32,128]{1,0:T(8,128)S(1)} %get-tuple-element.48, ...), kind=kOutput, calls=%fused_computation.91 | convolution fusion | flops 1065353216 | bytes 17281024 | tf_op jit(solution)/shard_map/av,vxy->axy/dot_general | solution.py:195
  608.0 54.9 %all-reduce.8.cloned.1.call-done = f32[20,32,128]{2,1,0:T(8,128)} async-done(((f32[20,32,128]{2,1,0:T(8,128)}), f32[20,32,128]{2,1,0:T(8,128)}) %all-reduce.8.cloned.1.call-update) | async-done | bytes 327696 | tf_op jit(solution)/shard_map/psum | solution.py:199
  669.2 19.1 %multiply_add_fusion = f32[1024,32,128]{0,2,1:T(8,128)} fusion(f32[1024,32,128]{0,2,1:T(8,128)} %copy-done.3, f32[32,128]{1,0:T(8,128)S(1)} %get-tuple-element.15, f32[32,128]{1,0:T(8,128)S(1)} %get-tuple-element.14, f32[20,32,128]{2,1,0:T(8,128)S(1)} %constant_dynamic-update-slice_fusion.40, f32[20,1024]{1,0:T(8,128)S(1)} %stack.12), kind=kOutput, calls=%fused_computation.90 | convolution fusion | flops 1019215872 | bytes 33996800 | tf_op jit(solution)/shard_map/av,axy->vxy/dot_general | solution.py:202
  688.3 17.4 %copy.32 = f32[1024,32,128]{2,1,0:T(8,128)} copy(f32[1024,32,128]{0,2,1:T(8,128)} %multiply_add_fusion) | data formatting | bytes 33554432 | tf_op jit(solution)/shard_map/add | solution.py:203
  (121 shorter events, 50.6 us)
Async XLA Ops:
  6.5 216.1 %all-reduce.4.cloned.1.call-start = ((), (), s32[]{:S(2)}) async-start(), calls=%async_computation | async-start | bytes 655360 | tf_op jit(solution)/shard_map/psum | solution.py:199
  26.9 43.7 %copy-start.5 = (f32[3,5,32,128]{3,2,1,0:T(8,128)S(1)}, f32[3,5,32,128]{3,2,1,0:T(8,128)}, u32[]{:S(2)}) copy-start(f32[3,5,32,128]{3,2,1,0:T(8,128)} %param.7) | copy-start | bytes 737284
  64.6 27.8 %collective-permute-start = (f32[1024,2,128]{0,2,1:T(8,128)}, f32[1024,2,128]{0,2,1:T(8,128)S(1)}, u32[]{:S(2)}, u32[]{:S(2)}) collective-permute-start(f32[1024,2,128]{0,2,1:T(8,128)} %get-tuple-element.44), channel_id=1, source_target_pairs={{8,0},{16,8},{24,16},{0,24},{9,1},{17,9},{25,17},{1,25},{10,2},{18... | collective-permute-start | bytes 3145736 | tf_op jit(solution)/shard_map/ppermute | solution.py:43
  68.5 46.1 %collective-permute-start.1 = (f32[1024,2,128]{0,2,1:T(8,128)S(1)}, f32[1024,2,128]{0,2,1:T(8,128)S(1)}, u32[]{:S(2)}, u32[]{:S(2)}) collective-permute-start(f32[1024,2,128]{0,2,1:T(8,128)S(1)} %get-tuple-element.45), channel_id=1, source_target_pairs={{0,8},{8,16},{16,24},{24,0},{1,9},{9,17},{17,25},{25,1},{2,10},{10... | collective-permute-start | bytes 3145736 | tf_op jit(solution)/shard_map/ppermute | solution.py:42
  114.6 27.7 %copy-start.13 = (f32[1,1024]{1,0:T(1,128)S(1)}, f32[1,1024]{1,0:T(1,128)}, u32[]{:S(2)}) copy-start(f32[1,1024]{1,0:T(1,128)} %get-tuple-element.88) | copy-start | bytes 12292
  114.6 27.7 %copy-start.14 = (f32[1,1024]{1,0:T(1,128)S(1)}, f32[1,1024]{1,0:T(1,128)}, u32[]{:S(2)}) copy-start(f32[1,1024]{1,0:T(1,128)} %get-tuple-element.89) | copy-start | bytes 12292
  114.6 27.7 %copy-start.15 = (f32[1,1024]{1,0:T(1,128)S(1)}, f32[1,1024]{1,0:T(1,128)}, u32[]{:S(2)}) copy-start(f32[1,1024]{1,0:T(1,128)} %get-tuple-element.90) | copy-start | bytes 12292
  142.2 23.4 %copy-start.2 = (f32[1024,32,128]{0,2,1:T(8,128)}, f32[1024,32,128]{0,2,1:T(8,128)S(1)}, u32[]{:S(2)}) copy-start(f32[1024,32,128]{0,2,1:T(8,128)S(1)} %fusion.38) | copy-start | bytes 50331652
  166.5 276.3 %all-reduce.6.cloned.1.call-start = ((), (), s32[]{:S(2)}) async-start(), calls=%async_computation.1 | async-start | bytes 655360 | tf_op jit(solution)/shard_map/psum | solution.py:199
  246.5 6.2 copy-start.1
  289.4 26.1 %collective-permute-start.2 = (f32[1024,2,128]{0,2,1:T(8,128)S(1)}, f32[1024,2,128]{0,2,1:T(8,128)S(1)}, u32[]{:S(2)}, u32[]{:S(2)}) collective-permute-start(f32[1024,2,128]{0,2,1:T(8,128)S(1)} %get-tuple-element.40), channel_id=1, source_target_pairs={{8,0},{16,8},{24,16},{0,24},{9,1},{17,9},{25,17},{1,25},{10,2},{18... | collective-permute-start | bytes 3145736 | tf_op jit(solution)/shard_map/ppermute | solution.py:43
  291.8 71.8 %copy-start.8 = (f32[32,128]{1,0:T(8,128)S(1)}, f32[32,128]{1,0:T(8,128)}, u32[]{:S(2)}) copy-start(f32[32,128]{1,0:T(8,128)} %get-tuple-element.49) | copy-start | bytes 49156
  291.8 71.9 %copy-start.9 = (f32[32,128]{1,0:T(8,128)S(1)}, f32[32,128]{1,0:T(8,128)}, u32[]{:S(2)}) copy-start(f32[32,128]{1,0:T(8,128)} %get-tuple-element.52) | copy-start | bytes 49156
  291.8 71.9 %copy-start.10 = (f32[32,128]{1,0:T(8,128)S(1)}, f32[32,128]{1,0:T(8,128)}, u32[]{:S(2)}) copy-start(f32[32,128]{1,0:T(8,128)} %get-tuple-element.53) | copy-start | bytes 49156
  291.8 71.9 %copy-start.11 = (f32[32,128]{1,0:T(8,128)S(1)}, f32[32,128]{1,0:T(8,128)}, u32[]{:S(2)}) copy-start(f32[32,128]{1,0:T(8,128)} %get-tuple-element.54) | copy-start | bytes 49156
  291.8 71.9 %copy-start.12 = (f32[32,128]{1,0:T(8,128)S(1)}, f32[32,128]{1,0:T(8,128)}, u32[]{:S(2)}) copy-start(f32[32,128]{1,0:T(8,128)} %get-tuple-element.59) | copy-start | bytes 49156
  291.8 44.1 %collective-permute-start.3 = (f32[1024,2,128]{0,2,1:T(8,128)S(1)}, f32[1024,2,128]{0,2,1:T(8,128)S(1)}, u32[]{:S(2)}, u32[]{:S(2)}) collective-permute-start(f32[1024,2,128]{0,2,1:T(8,128)S(1)} %get-tuple-element.41), channel_id=1, source_target_pairs={{0,8},{8,16},{16,24},{24,0},{1,9},{9,17},{17,25},{25,1},{2,10},{10... | collective-permute-start | bytes 3145736 | tf_op jit(solution)/shard_map/ppermute | solution.py:42
  363.6 23.5 %copy-start.4 = (f32[1024,32,128]{0,2,1:T(8,128)}, f32[1024,32,128]{0,2,1:T(8,128)S(1)}, u32[]{:S(2)}) copy-start(f32[1024,32,128]{0,2,1:T(8,128)S(1)} %fusion.22) | copy-start | bytes 50331652
  387.9 275.0 %all-reduce.8.cloned.1.call-start = ((), (), s32[]{:S(2)}) async-start(), calls=%async_computation.2 | async-start | bytes 655360 | tf_op jit(solution)/shard_map/psum | solution.py:199
  509.5 26.1 %collective-permute-start.4 = (f32[1024,2,128]{0,2,1:T(8,128)S(1)}, f32[1024,2,128]{0,2,1:T(8,128)S(1)}, u32[]{:S(2)}, u32[]{:S(2)}) collective-permute-start(f32[1024,2,128]{0,2,1:T(8,128)S(1)} %get-tuple-element.36), channel_id=1, source_target_pairs={{8,0},{16,8},{24,16},{0,24},{9,1},{17,9},{25,17},{1,25},{10,2},{18... | collective-permute-start | bytes 3145736 | tf_op jit(solution)/shard_map/ppermute | solution.py:43
  511.9 71.8 %copy-start.6 = (f32[32,128]{1,0:T(8,128)S(1)}, f32[32,128]{1,0:T(8,128)}, u32[]{:S(2)}) copy-start(f32[32,128]{1,0:T(8,128)} %get-tuple-element.61) | copy-start | bytes 49156
  511.9 71.9 %copy-start.7 = (f32[32,128]{1,0:T(8,128)S(1)}, f32[32,128]{1,0:T(8,128)}, u32[]{:S(2)}) copy-start(f32[32,128]{1,0:T(8,128)} %get-tuple-element.62) | copy-start | bytes 49156
  511.9 44.2 %collective-permute-start.5 = (f32[1024,2,128]{0,2,1:T(8,128)S(1)}, f32[1024,2,128]{0,2,1:T(8,128)S(1)}, u32[]{:S(2)}, u32[]{:S(2)}) collective-permute-start(f32[1024,2,128]{0,2,1:T(8,128)S(1)} %get-tuple-element.37), channel_id=1, source_target_pairs={{0,8},{8,16},{16,24},{24,0},{1,9},{9,17},{17,25},{25,1},{2,10},{10... | collective-permute-start | bytes 3145736 | tf_op jit(solution)/shard_map/ppermute | solution.py:42
  583.7 23.4 %copy-start.3 = (f32[1024,32,128]{0,2,1:T(8,128)}, f32[1024,32,128]{0,2,1:T(8,128)S(1)}, u32[]{:S(2)}) copy-start(f32[1024,32,128]{0,2,1:T(8,128)S(1)} %fusion.6) | copy-start | bytes 50331652
  (1 other events, 6.2 us)
Sparse Core Ops, SparseCore 0:
  166.6 55.9 all-reduce.3
  388.0 54.6 all-reduce.5
  608.1 54.6 all-reduce.7
where the time goes:
time: 724 us; the launch traced here: 713 us
  waiting for transfers between devices  296 us (41%)
  other arithmetic  210 us (29%)
  matrix products  124 us (17%)
  local copies, waits for them, and re-layouts  58.5 us (8%)
  between operations  14.2 us (2%)
  starting transfers between devices  10 us (1%)
    sub x6, other arithmetic, upwind_back(): return center - 0.5 * lam_col * (3.0 * center - 4.0 * nearer + farther)  187 us
    psum x3, waiting for transfers between devices, shards(): summed = lax.psum(raw_moments, 'vel')  165 us
    dot_general x3, matrix products, shards(): jnp.einsum('av,vxy->axy', table, weight * advected, precision=lax.Precisi...  70.1 us
    ppermute x3, waiting for transfers between devices, with_halo(): after = lax.ppermute(first, axis, down)  67.8 us
    ppermute x3, waiting for transfers between devices, with_halo(): before = lax.ppermute(last, axis, up)  63.2 us
    dot_general x3, matrix products, shards(): jnp.einsum('av,axy->vxy', table, coeffs, precision=lax.Precision.HIGHEST)  54.2 us
    unnamed x36, local copies, waits for them, and re-layouts  28.9 us
    unnamed x54, other arithmetic  18.7 us
  transfers between devices with their start and end apart: 9, of which 9 were waited for; matrix products, arithmetic and copies ran while one was open for 0% of the time, Pallas kernels for 0%

commit v1 on v0

--- a/solution.py
+++ b/solution.py
@@ -1,8 +1,10 @@
+import functools
 import math
 import jax
 import jax.numpy as jnp
 from jax import lax
 from jax.sharding import PartitionSpec as P
+from jax.lax import axis_size, ppermute
 
 SPEED_POINTS = 8192
 STEPS = 3
@@ -30,6 +32,19 @@
     for second in range(degree - first, -1, -1)
 ]
 monomial_place = {exponents: place for place, exponents in enumerate(monomials)}
+
+
+def _save_halves(xx, mesh_ax):
+    many = axis_size(mesh_ax)
+    raw_out = xx
+    known = lambda opened: [(kk, kk ^ opened) for kk in range(many)]
+    for k0 in range(many.bit_length() - 1):
+        reached = ppermute(raw_out, axis_name=mesh_ax, perm=known(1 << k0))
+        raw_out = raw_out + reached
+    return raw_out
+
+
+watch_sides_on_mesh = functools.partial(_save_halves, mesh_ax="vel")
 
 
 def with_halo(x, sides, width):
@@ -196,7 +211,7 @@
             "av,vxy->axy", table, weight * advected, precision=lax.Precision.HIGHEST
         )
         zero_cells = jnp.zeros_like(particle_concentration)
-        summed = lax.psum(raw_moments, "vel")
+        summed = watch_sides_on_mesh(raw_moments)
         polys = hermite_polys(flow_rows, reciprocal_factor)
         coeffs = to_coeffs(to_modes(summed, polys, zero_cells), polys, zero_cells)
         returned = jnp.einsum("av,axy->vxy", table, coeffs, precision=lax.Precision.HIGHEST)

time: 724 us -> 606 us (0.84)
  waiting for transfers between devices: 296 us -> 205 us
  other arithmetic: 210 us -> 193 us
  starting transfers between devices: 10 us -> 23.7 us
  between operations: 14.2 us -> 0.92 us
    psum x3 -> x0, waiting for transfers between devices: 165 us -> none  [shards(): summed = lax.psum(raw_moments, 'vel')]
    ppermute x0 -> x9, waiting for transfers between devices: none -> 72.3 us  [_save_halves(): reached = ppermute(raw_out, axis_name=mesh_ax, perm=known(1 << k0))]
    unnamed x54, other arithmetic: 18.7 us -> 1.73 us
    ppermute x0 -> x9, starting transfers between devices: none -> 14.8 us  [_save_halves(): reached = ppermute(raw_out, axis_name=mesh_ax, perm=known(1 << k0))]
    unnamed x36 -> x26, local copies, waits for them, and re-layouts: 28.9 us -> 28.9 us
  transfers between devices with their start and end apart: 9 -> 15, of which waited for: 9 -> 15; matrix products, arithmetic and copies ran while one was open for 0% -> 0% of each run, Pallas kernels for 0% -> 0%
where the time goes in v1:
time: 606 us; the launch traced here: 601 us
  waiting for transfers between devices  205 us (34%)
  other arithmetic  193 us (32%)
  matrix products  123 us (20%)
  local copies, waits for them, and re-layouts  56.3 us (9%)
  starting transfers between devices  23.7 us (4%)
    sub x6, other arithmetic, upwind_back(): return center - 0.5 * lam_col * (3.0 * center - 4.0 * nearer + farther)  188 us
    ppermute x9, waiting for transfers between devices, _save_halves(): reached = ppermute(raw_out, axis_name=mesh_ax, perm=known(1 << k0))  72.3 us
    dot_general x3, matrix products, shards(): jnp.einsum('av,vxy->axy', table, weight * advected, precision=lax.Precisi...  70.1 us
    ppermute x3, waiting for transfers between devices, with_halo(): after = lax.ppermute(first, axis, down)  68.2 us
    ppermute x3, waiting for transfers between devices, with_halo(): before = lax.ppermute(last, axis, up)  64.2 us
    dot_general x3, matrix products, shards(): jnp.einsum('av,axy->vxy', table, coeffs, precision=lax.Precision.HIGHEST)  52.6 us
    unnamed x26, local copies, waits for them, and re-layouts  28.9 us
    add x1, local copies, waits for them, and re-layouts, shards(): adjoint = (1.0 - relaxation_rate) * advected + relaxation_rate * returned  17.4 us
  transfers between devices with their start and end apart: 15, of which 15 were waited for; matrix products, arithmetic and copies ran while one was open for 0% of the time, Pallas kernels for 0%

profile of v1, /device:TPU:0, one launch (start us, length us, event | category | flops | bytes accessed | tf_op | source)
XLA Modules:
  0.0 601.5 jit_solution(15012369917515756597)
XLA Ops:
  1.5 16.5 %copy.21 = f32[1024,32,128]{0,2,1:T(8,128)} copy(f32[1024,32,128]{2,1,0:T(8,128)} %param.4) | data formatting | bytes 33554432 | tf_op args[0]
  20.4 34.8 %fusion.46 = f32[1024,32,128]{0,2,1:T(8,128)} fusion(f32[1024,32,128]{0,2,1:T(8,128)} %copy.21, f32[1024,32,2]{0,2,1:T(2,128)S(1)} %get-tuple-element.47, f32[1024,32,2]{0,2,1:T(2,128)S(1)} %get-tuple-element.46, f32[1024]{0:T(1024)S(1)} %bitcast.1794, pred[1024]{0:T(1024)(128)(4,1)S(1)} %get-tuple-element.6), kind=kLoop, calls=%fused_computation.70 | loop fusion | flops 50331648 | bytes 34083840 | tf_op jit(solution)/shard_map/sub | solution.py:166
  65.2 20.6 %collective-permute-done = f32[1024,2,128]{0,2,1:T(8,128)S(1)} collective-permute-done((f32[1024,2,128]{0,2,1:T(8,128)}, f32[1024,2,128]{0,2,1:T(8,128)S(1)}, u32[]{:S(2)}, u32[]{:S(2)}) %collective-permute-start) | collective-permute-done | bytes 1048608 | tf_op jit(solution)/shard_map/ppermute | solution.py:58
  85.8 22.2 %collective-permute-done.1 = f32[1024,2,128]{0,2,1:T(8,128)S(1)} collective-permute-done((f32[1024,2,128]{0,2,1:T(8,128)S(1)}, f32[1024,2,128]{0,2,1:T(8,128)S(1)}, u32[]{:S(2)}, u32[]{:S(2)}) %collective-permute-start.1) | collective-permute-done | bytes 1048608 | tf_op jit(solution)/shard_map/ppermute | solution.py:57
  108.0 27.6 %fusion.38 = f32[1024,32,128]{0,2,1:T(8,128)S(1)} fusion(f32[1024,32,128]{0,2,1:T(8,128)} %fusion.46, f32[1024,2,128]{0,2,1:T(8,128)S(1)} %collective-permute-done.1, f32[1024,2,128]{0,2,1:T(8,128)S(1)} %collective-permute-done, f32[1024]{0:T(1024)S(1)} %bitcast.1791, pred[1024]{0:T(1024)(128)(4,1)S(1)} %get-tuple-element.5), kind=kLoop, calls=%fused_computation.62 | loop fusion | flops 50331648 | bytes 35656704 | tf_op jit(solution)/shard_map/sub | solution.py:166
  135.7 23.4 %fusion.86 = f32[20,32,128]{2,0,1:T(8,128)S(1)} fusion(f32[1024,32,128]{0,2,1:T(8,128)S(1)} %fusion.38, f32[32,128]{1,0:T(8,128)S(1)} %get-tuple-element.55, f32[1024]{0:T(1024)S(1)} %bitcast.1803, f32[32,128]{1,0:T(8,128)S(1)} %get-tuple-element.56, f32[1024]{0:T(1024)S(1)} %bitcast.1800, f32[32,128]{1,0:T(8,128)S(1)} %get-tuple-element.58, ...), kind=kOutput, calls=%fused_computation.125 | convolution fusion | flops 1065353216 | bytes 17281024 | tf_op jit(solution)/shard_map/av,vxy->axy/dot_general | solution.py:210
  162.5 8.2 %collective-permute-done.3 = f32[20,32,128]{2,1,0:T(8,128)S(1)} collective-permute-done((f32[20,32,128]{2,1,0:T(8,128)S(1)}, f32[20,32,128]{2,1,0:T(8,128)S(1)}, u32[]{:S(2)}, u32[]{:S(2)}) %collective-permute-start.3) | collective-permute-done | bytes 327712 | tf_op jit(solution)/shard_map/ppermute | solution.py:42
  173.4 14.2 %collective-permute-done.4 = f32[20,32,128]{2,1,0:T(8,128)S(1)} collective-permute-done((f32[20,32,128]{2,1,0:T(8,128)S(1)}, f32[20,32,128]{2,1,0:T(8,128)S(1)}, u32[]{:S(2)}, u32[]{:S(2)}) %collective-permute-start.4) | collective-permute-done | bytes 327712 | tf_op jit(solution)/shard_map/ppermute | solution.py:42
  188.4 17.5 %multiply_add_fusion.2 = f32[1024,32,128]{0,2,1:T(8,128)S(1)} fusion(f32[1024,32,128]{0,2,1:T(8,128)} %copy-done.2, f32[32,128]{1,0:T(8,128)S(1)} %get-tuple-element.64, f32[32,128]{1,0:T(8,128)S(1)} %get-tuple-element.63, f32[20,32,128]{2,1,0:T(8,128)S(1)} %constant_dynamic-update-slice_fusion, f32[20,1024]{1,0:T(8,128)S(1)} %stack.12), kind=kOutput, calls=%fused_computation.124 | convolution fusion | flops 1019215872 | bytes 33996800 | tf_op jit(solution)/shard_map/av,axy->vxy/dot_general | solution.py:217
  212.3 35.0 %fusion.30 = f32[1024,32,128]{0,2,1:T(8,128)} fusion(f32[1024,32,128]{0,2,1:T(8,128)} %copy-done.1, f32[1024,32,2]{0,2,1:T(2,128)S(1)} %get-tuple-element.43, f32[1024,32,2]{0,2,1:T(2,128)S(1)} %get-tuple-element.42, f32[1024]{0:T(1024)S(1)} %bitcast.1795, pred[1024]{0:T(1024)(128)(4,1)S(1)} %get-tuple-element.6), kind=kLoop, calls=%fused_computation.54 | loop fusion | flops 50331648 | bytes 34083840 | tf_op jit(solution)/shard_map/sub | solution.py:166
  251.0 24.0 %collective-permute-done.5 = f32[1024,2,128]{0,2,1:T(8,128)S(1)} collective-permute-done((f32[1024,2,128]{0,2,1:T(8,128)S(1)}, f32[1024,2,128]{0,2,1:T(8,128)S(1)}, u32[]{:S(2)}, u32[]{:S(2)}) %collective-permute-start.5) | collective-permute-done | bytes 1048608 | tf_op jit(solution)/shard_map/ppermute | solution.py:58
  275.0 20.3 %collective-permute-done.6 = f32[1024,2,128]{0,2,1:T(8,128)S(1)} collective-permute-done((f32[1024,2,128]{0,2,1:T(8,128)S(1)}, f32[1024,2,128]{0,2,1:T(8,128)S(1)}, u32[]{:S(2)}, u32[]{:S(2)}) %collective-permute-start.6) | collective-permute-done | bytes 1048608 | tf_op jit(solution)/shard_map/ppermute | solution.py:57
  295.4 27.6 %fusion.22 = f32[1024,32,128]{0,2,1:T(8,128)S(1)} fusion(f32[1024,32,128]{0,2,1:T(8,128)} %fusion.30, f32[1024,2,128]{0,2,1:T(8,128)S(1)} %collective-permute-done.6, f32[1024,2,128]{0,2,1:T(8,128)S(1)} %collective-permute-done.5, f32[1024]{0:T(1024)S(1)} %bitcast.1792, pred[1024]{0:T(1024)(128)(4,1)S(1)} %get-tuple-element.5), kind=kLoop, calls=%fused_computation.46 | loop fusion | flops 50331648 | bytes 35656704 | tf_op jit(solution)/shard_map/sub | solution.py:166
  323.0 23.4 %fusion.70 = f32[20,32,128]{2,0,1:T(8,128)S(1)} fusion(f32[1024,32,128]{0,2,1:T(8,128)S(1)} %fusion.22, f32[32,128]{1,0:T(8,128)S(1)} %get-tuple-element.52, f32[32,128]{1,0:T(8,128)S(1)} %copy-done.5, f32[32,128]{1,0:T(8,128)S(1)} %copy-done.7, f32[32,128]{1,0:T(8,128)S(1)} %copy-done.6, f32[32,128]{1,0:T(8,128)S(1)} %get-tuple-element.49, ...), kind=kOutput, calls=%fused_computation.108 | convolution fusion | flops 1065353216 | bytes 17281024 | tf_op jit(solution)/shard_map/av,vxy->axy/dot_general | solution.py:210
  361.6 14.5 %collective-permute-done.9 = f32[20,32,128]{2,1,0:T(8,128)S(1)} collective-permute-done((f32[20,32,128]{2,1,0:T(8,128)S(1)}, f32[20,32,128]{2,1,0:T(8,128)S(1)}, u32[]{:S(2)}, u32[]{:S(2)}) %collective-permute-start.9) | collective-permute-done | bytes 327712 | tf_op jit(solution)/shard_map/ppermute | solution.py:42
  376.8 17.5 %multiply_add_fusion.1 = f32[1024,32,128]{0,2,1:T(8,128)S(1)} fusion(f32[1024,32,128]{0,2,1:T(8,128)} %copy-done.3, f32[32,128]{1,0:T(8,128)S(1)} %get-tuple-element.66, f32[32,128]{1,0:T(8,128)S(1)} %get-tuple-element.65, f32[20,32,128]{2,1,0:T(8,128)S(1)} %constant_dynamic-update-slice_fusion.20, f32[20,1024]{1,0:T(8,128)S(1)} %stack.12), kind=kOutput, calls=%fused_computation.107 | convolution fusion | flops 1019215872 | bytes 33996800 | tf_op jit(solution)/shard_map/av,axy->vxy/dot_general | solution.py:217
  400.7 35.0 %fusion.14 = f32[1024,32,128]{0,2,1:T(8,128)} fusion(f32[1024,32,128]{0,2,1:T(8,128)} %copy-done, f32[1024,32,2]{0,2,1:T(2,128)S(1)} %get-tuple-element.39, f32[1024,32,2]{0,2,1:T(2,128)S(1)} %get-tuple-element.38, f32[1024]{0:T(1024)S(1)} %bitcast.1796, pred[1024]{0:T(1024)(128)(4,1)S(1)} %get-tuple-element.6), kind=kLoop, calls=%fused_computation.38 | loop fusion | flops 50331648 | bytes 34083840 | tf_op jit(solution)/shard_map/sub | solution.py:166
  439.9 23.6 %collective-permute-done.10 = f32[1024,2,128]{0,2,1:T(8,128)S(1)} collective-permute-done((f32[1024,2,128]{0,2,1:T(8,128)S(1)}, f32[1024,2,128]{0,2,1:T(8,128)S(1)}, u32[]{:S(2)}, u32[]{:S(2)}) %collective-permute-start.10) | collective-permute-done | bytes 1048608 | tf_op jit(solution)/shard_map/ppermute | solution.py:58
  463.5 21.6 %collective-permute-done.11 = f32[1024,2,128]{0,2,1:T(8,128)S(1)} collective-permute-done((f32[1024,2,128]{0,2,1:T(8,128)S(1)}, f32[1024,2,128]{0,2,1:T(8,128)S(1)}, u32[]{:S(2)}, u32[]{:S(2)}) %collective-permute-start.11) | collective-permute-done | bytes 1048608 | tf_op jit(solution)/shard_map/ppermute | solution.py:57
  485.1 27.6 %fusion.6 = f32[1024,32,128]{0,2,1:T(8,128)S(1)} fusion(f32[1024,32,128]{0,2,1:T(8,128)} %fusion.14, f32[1024,2,128]{0,2,1:T(8,128)S(1)} %collective-permute-done.11, f32[1024,2,128]{0,2,1:T(8,128)S(1)} %collective-permute-done.10, f32[1024]{0:T(1024)S(1)} %bitcast.1793, pred[1024]{0:T(1024)(128)(4,1)S(1)} %get-tuple-element.5), kind=kLoop, calls=%fused_computation.30 | loop fusion | flops 50331648 | bytes 35656704 | tf_op jit(solution)/shard_map/sub | solution.py:166
  512.7 23.4 %fusion.54 = f32[20,32,128]{2,0,1:T(8,128)S(1)} fusion(f32[1024,32,128]{0,2,1:T(8,128)S(1)} %fusion.6, f32[32,128]{1,0:T(8,128)S(1)} %get-tuple-element.61, f32[32,128]{1,0:T(8,128)S(1)} %get-tuple-element.62, f32[32,128]{1,0:T(8,128)S(1)} %get-tuple-element.60, f32[32,128]{1,0:T(8,128)S(1)} %get-tuple-element.51, f32[32,128]{1,0:T(8,128)S(1)} %get-tuple-element.48, ...), kind=kOutput, calls=%fused_computation.91 | convolution fusion | flops 1065353216 | bytes 17281024 | tf_op jit(solution)/shard_map/av,vxy->axy/dot_general | solution.py:210
  551.1 14.5 %collective-permute-done.14 = f32[20,32,128]{2,1,0:T(8,128)S(1)} collective-permute-done((f32[20,32,128]{2,1,0:T(8,128)S(1)}, f32[20,32,128]{2,1,0:T(8,128)S(1)}, u32[]{:S(2)}, u32[]{:S(2)}) %collective-permute-start.14) | collective-permute-done | bytes 327712 | tf_op jit(solution)/shard_map/ppermute | solution.py:42
  566.3 17.6 %multiply_add_fusion = f32[1024,32,128]{0,2,1:T(8,128)} fusion(f32[1024,32,128]{0,2,1:T(8,128)S(1)} %fusion.6, f32[32,128]{1,0:T(8,128)S(1)} %get-tuple-element.15, f32[32,128]{1,0:T(8,128)S(1)} %get-tuple-element.14, f32[20,32,128]{2,1,0:T(8,128)S(1)} %constant_dynamic-update-slice_fusion.40, f32[20,1024]{1,0:T(8,128)S(1)} %stack.12), kind=kOutput, calls=%fused_computation.90 | convolution fusion | flops 1019215872 | bytes 33996800 | tf_op jit(solution)/shard_map/av,axy->vxy/dot_general | solution.py:217
  583.9 17.4 %copy.35 = f32[1024,32,128]{2,1,0:T(8,128)} copy(f32[1024,32,128]{0,2,1:T(8,128)} %multiply_add_fusion) | data formatting | bytes 33554432 | tf_op jit(solution)/shard_map/add | solution.py:218
  (129 shorter events, 72.9 us)
Async XLA Ops:
  20.4 44.2 %copy-start.4 = (f32[3,5,32,128]{3,2,1,0:T(8,128)S(1)}, f32[3,5,32,128]{3,2,1,0:T(8,128)}, u32[]{:S(2)}) copy-start(f32[3,5,32,128]{3,2,1,0:T(8,128)} %param.7) | copy-start | bytes 737284
  58.0 27.8 %collective-permute-start = (f32[1024,2,128]{0,2,1:T(8,128)}, f32[1024,2,128]{0,2,1:T(8,128)S(1)}, u32[]{:S(2)}, u32[]{:S(2)}) collective-permute-start(f32[1024,2,128]{0,2,1:T(8,128)} %get-tuple-element.44), channel_id=1, source_target_pairs={{8,0},{16,8},{24,16},{0,24},{9,1},{17,9},{25,17},{1,25},{10,2},{18... | collective-permute-start | bytes 3145736 | tf_op jit(solution)/shard_map/ppermute | solution.py:58
  61.9 46.1 %collective-permute-start.1 = (f32[1024,2,128]{0,2,1:T(8,128)S(1)}, f32[1024,2,128]{0,2,1:T(8,128)S(1)}, u32[]{:S(2)}, u32[]{:S(2)}) collective-permute-start(f32[1024,2,128]{0,2,1:T(8,128)S(1)} %get-tuple-element.45), channel_id=1, source_target_pairs={{0,8},{8,16},{16,24},{24,0},{1,9},{9,17},{17,25},{25,1},{2,10},{10... | collective-permute-start | bytes 3145736 | tf_op jit(solution)/shard_map/ppermute | solution.py:57
  108.0 27.6 %copy-start.8 = (f32[1,1024]{1,0:T(1,128)S(1)}, f32[1,1024]{1,0:T(1,128)}, u32[]{:S(2)}) copy-start(f32[1,1024]{1,0:T(1,128)} %get-tuple-element.88) | copy-start | bytes 12292
  108.0 27.6 %copy-start.9 = (f32[1,1024]{1,0:T(1,128)S(1)}, f32[1,1024]{1,0:T(1,128)}, u32[]{:S(2)}) copy-start(f32[1,1024]{1,0:T(1,128)} %get-tuple-element.89) | copy-start | bytes 12292
  108.0 27.6 %copy-start.10 = (f32[1,1024]{1,0:T(1,128)S(1)}, f32[1,1024]{1,0:T(1,128)}, u32[]{:S(2)}) copy-start(f32[1,1024]{1,0:T(1,128)} %get-tuple-element.90) | copy-start | bytes 12292
  135.6 23.4 %copy-start.2 = (f32[1024,32,128]{0,2,1:T(8,128)}, f32[1024,32,128]{0,2,1:T(8,128)S(1)}, u32[]{:S(2)}) copy-start(f32[1024,32,128]{0,2,1:T(8,128)S(1)} %fusion.38) | copy-start | bytes 50331652
  159.1 1.7 collective-permute-start.2
  160.9 9.8 %collective-permute-start.3 = (f32[20,32,128]{2,1,0:T(8,128)S(1)}, f32[20,32,128]{2,1,0:T(8,128)S(1)}, u32[]{:S(2)}, u32[]{:S(2)}) collective-permute-start(f32[20,32,128]{2,1,0:T(8,128)S(1)} %copy_add_fusion.2), channel_id=1, source_target_pairs={{0,2},{1,3},{2,0},{3,1},{4,6},{5,7},{6,4},{7,5},{8,10},{9,11},{10,... | collective-permute-start | bytes 983048 | tf_op jit(solution)/shard_map/ppermute | solution.py:42
  170.7 16.9 %collective-permute-start.4 = (f32[20,32,128]{2,1,0:T(8,128)S(1)}, f32[20,32,128]{2,1,0:T(8,128)S(1)}, u32[]{:S(2)}, u32[]{:S(2)}) collective-permute-start(f32[20,32,128]{2,1,0:T(8,128)S(1)} %add.3972), channel_id=1, source_target_pairs={{0,4},{1,5},{2,6},{3,7},{4,0},{5,1},{6,2},{7,3},{8,12},{9,13},{10,... | collective-permute-start | bytes 983048 | tf_op jit(solution)/shard_map/ppermute | solution.py:42
  249.0 26.1 %collective-permute-start.5 = (f32[1024,2,128]{0,2,1:T(8,128)S(1)}, f32[1024,2,128]{0,2,1:T(8,128)S(1)}, u32[]{:S(2)}, u32[]{:S(2)}) collective-permute-start(f32[1024,2,128]{0,2,1:T(8,128)S(1)} %get-tuple-element.40), channel_id=1, source_target_pairs={{8,0},{16,8},{24,16},{0,24},{9,1},{17,9},{25,17},{1,25},{10,2},{18... | collective-permute-start | bytes 3145736 | tf_op jit(solution)/shard_map/ppermute | solution.py:58
  250.4 72.5 %copy-start.5 = (f32[32,128]{1,0:T(8,128)S(1)}, f32[32,128]{1,0:T(8,128)}, u32[]{:S(2)}) copy-start(f32[32,128]{1,0:T(8,128)} %get-tuple-element.53) | copy-start | bytes 49156
  250.5 72.6 %copy-start.6 = (f32[32,128]{1,0:T(8,128)S(1)}, f32[32,128]{1,0:T(8,128)}, u32[]{:S(2)}) copy-start(f32[32,128]{1,0:T(8,128)} %get-tuple-element.54) | copy-start | bytes 49156
  250.5 72.6 %copy-start.7 = (f32[32,128]{1,0:T(8,128)S(1)}, f32[32,128]{1,0:T(8,128)}, u32[]{:S(2)}) copy-start(f32[32,128]{1,0:T(8,128)} %get-tuple-element.59) | copy-start | bytes 49156
  250.5 44.9 %collective-permute-start.6 = (f32[1024,2,128]{0,2,1:T(8,128)S(1)}, f32[1024,2,128]{0,2,1:T(8,128)S(1)}, u32[]{:S(2)}, u32[]{:S(2)}) collective-permute-start(f32[1024,2,128]{0,2,1:T(8,128)S(1)} %get-tuple-element.41), channel_id=1, source_target_pairs={{0,8},{8,16},{16,24},{24,0},{1,9},{9,17},{17,25},{25,1},{2,10},{10... | collective-permute-start | bytes 3145736 | tf_op jit(solution)/shard_map/ppermute | solution.py:57
  323.0 23.4 %copy-start.3 = (f32[1024,32,128]{0,2,1:T(8,128)}, f32[1024,32,128]{0,2,1:T(8,128)S(1)}, u32[]{:S(2)}) copy-start(f32[1024,32,128]{0,2,1:T(8,128)S(1)} %fusion.22) | copy-start | bytes 50331652
  346.5 1.7 collective-permute-start.7
  348.3 9.9 %collective-permute-start.8 = (f32[20,32,128]{2,1,0:T(8,128)S(1)}, f32[20,32,128]{2,1,0:T(8,128)S(1)}, u32[]{:S(2)}, u32[]{:S(2)}) collective-permute-start(f32[20,32,128]{2,1,0:T(8,128)S(1)} %copy_add_fusion.1), channel_id=1, source_target_pairs={{0,2},{1,3},{2,0},{3,1},{4,6},{5,7},{6,4},{7,5},{8,10},{9,11},{10,... | collective-permute-start | bytes 983048 | tf_op jit(solution)/shard_map/ppermute | solution.py:42
  358.2 17.9 %collective-permute-start.9 = (f32[20,32,128]{2,1,0:T(8,128)S(1)}, f32[20,32,128]{2,1,0:T(8,128)S(1)}, u32[]{:S(2)}, u32[]{:S(2)}) collective-permute-start(f32[20,32,128]{2,1,0:T(8,128)S(1)} %add.4112), channel_id=1, source_target_pairs={{0,4},{1,5},{2,6},{3,7},{4,0},{5,1},{6,2},{7,3},{8,12},{9,13},{10,... | collective-permute-start | bytes 983048 | tf_op jit(solution)/shard_map/ppermute | solution.py:42
  437.4 26.1 %collective-permute-start.10 = (f32[1024,2,128]{0,2,1:T(8,128)S(1)}, f32[1024,2,128]{0,2,1:T(8,128)S(1)}, u32[]{:S(2)}, u32[]{:S(2)}) collective-permute-start(f32[1024,2,128]{0,2,1:T(8,128)S(1)} %get-tuple-element.36), channel_id=1, source_target_pairs={{8,0},{16,8},{24,16},{0,24},{9,1},{17,9},{25,17},{1,25},{10,2},{18... | collective-permute-start | bytes 3145736 | tf_op jit(solution)/shard_map/ppermute | solution.py:58
  439.9 45.2 %collective-permute-start.11 = (f32[1024,2,128]{0,2,1:T(8,128)S(1)}, f32[1024,2,128]{0,2,1:T(8,128)S(1)}, u32[]{:S(2)}, u32[]{:S(2)}) collective-permute-start(f32[1024,2,128]{0,2,1:T(8,128)S(1)} %get-tuple-element.37), channel_id=1, source_target_pairs={{0,8},{8,16},{16,24},{24,0},{1,9},{9,17},{17,25},{25,1},{2,10},{10... | collective-permute-start | bytes 3145736 | tf_op jit(solution)/shard_map/ppermute | solution.py:57
  536.1 1.7 collective-permute-start.12
  537.9 9.8 %collective-permute-start.13 = (f32[20,32,128]{2,1,0:T(8,128)S(1)}, f32[20,32,128]{2,1,0:T(8,128)S(1)}, u32[]{:S(2)}, u32[]{:S(2)}) collective-permute-start(f32[20,32,128]{2,1,0:T(8,128)S(1)} %copy_add_fusion), channel_id=1, source_target_pairs={{0,2},{1,3},{2,0},{3,1},{4,6},{5,7},{6,4},{7,5},{8,10},{9,11},{10,... | collective-permute-start | bytes 983048 | tf_op jit(solution)/shard_map/ppermute | solution.py:42
  547.8 17.8 %collective-permute-start.14 = (f32[20,32,128]{2,1,0:T(8,128)S(1)}, f32[20,32,128]{2,1,0:T(8,128)S(1)}, u32[]{:S(2)}, u32[]{:S(2)}) collective-permute-start(f32[20,32,128]{2,1,0:T(8,128)S(1)} %add.4252), channel_id=1, source_target_pairs={{0,4},{1,5},{2,6},{3,7},{4,0},{5,1},{6,2},{7,3},{8,12},{9,13},{10,... | collective-permute-start | bytes 983048 | tf_op jit(solution)/shard_map/ppermute | solution.py:42
  (2 other events, 12.3 us)
